TPU v7x, 128 devices: a whole 4x4x4 slice. The times are simulated.
128 devices in a mesh: band: 16 (over x, z_lo, core), grid: 8 (over y, z_hi).
Axes of the slice: x: 4, y: 4, z: 4 (z_hi: 2, z_lo: 2; z = z_hi * 2 + z_lo), core: 2. Of those that a mesh axis runs over, the one named last changes fastest.
Arguments:
- valence: bfloat16 [32, 2, 160, 160, 160], P('band', None, 'grid'), may hold values from -6 to 6
- conduction: bfloat16 [16, 2, 160, 160, 160], P('band', None, 'grid'), may hold values from -6 to 6
- val_energy: float32 [32], replicated, may hold values from -12 to -1
- cond_energy: float32 [16], replicated, may hold values from 1 to 16
- cond_band: int32 [16], P('band'), may hold values from 0 to 15, each once
- owners: int32 [2], replicated, may hold values from 0 to 15
- gvectors: int32 [3, 4096], replicated, may hold values from 0 to 159, as said below
Outputs:
- chi0: float32 [2, 4096, 4096], P(None, 'grid', 'band')
Inputs may be any that keep to these rules, and one draw needn't show every extreme that they name: `gvectors`: the G-vectors are distinct; each component, read between -80 and 80, lies within -10 to 10. `owners`: each entry is an index along band. `cond_band`: A permutation of the global conduction band numbers.
All inputs are finite; a program needn't handle non-finite values.
Results may differ from a plain program's by a relative error of at most 0.0092.
Values may be sent and summed in bfloat16 or wider, within the bound.
No kernel may reach another device: no remote copies, remote signals or barrier semaphores. Data moves between devices by JAX's collectives and lax.ppermute only.
A program may use at most 192 MiB of HBM per device.

v0:
```python
import math
import jax
import jax.numpy as jnp
from jax import lax
from jax.sharding import PartitionSpec as P

ROUNDS = 2


def from_root(block, axis, owner):
    block = jnp.where(lax.axis_index(axis) == owner, block, jnp.zeros_like(block))
    return lax.psum(block, axis)


def dft_tables(length):
    positions = jnp.arange(length, dtype=jnp.int32)
    phase_index = positions[:, None] * positions[None, :] % length
    angles = phase_index.astype(jnp.float32) * (2.0 * math.pi / length)
    return (jnp.cos(angles).astype(jnp.bfloat16), jnp.sin(angles).astype(jnp.bfloat16))


def wide_table(cos_table, sin_table):
    top_half = jnp.concatenate([cos_table, -sin_table], axis=1)
    low_half = jnp.concatenate([sin_table, cos_table], axis=1)
    return jnp.concatenate([top_half, low_half], axis=0)


def plane_transform(density, wide, cos_table, sin_table):
    length = cos_table.shape[0]
    along_z = jnp.einsum("bxyk,kq->bxyq", density, wide, preferred_element_type=jnp.float32).astype(
        jnp.bfloat16
    )
    cos_part = jnp.einsum("bxyk,yq->bxqk", along_z, cos_table, preferred_element_type=jnp.float32)
    sin_part = jnp.einsum("bxyk,yq->bxqk", along_z, sin_table, preferred_element_type=jnp.float32)
    real_part = cos_part[..., :length] + sin_part[..., length:]
    imag_part = cos_part[..., length:] - sin_part[..., :length]
    return jnp.concatenate([real_part, imag_part], axis=-1).astype(jnp.bfloat16)


def shards(valence, conduction, val_energy, cond_energy, cond_band, owners, gvectors):
    val_dev = valence.shape[0]
    cond_dev = conduction.shape[0]
    x_local = valence.shape[2]
    length = valence.shape[3]
    y_local = length // lax.axis_size("grid")
    grid_pos = lax.axis_index("grid")
    band_pos = lax.axis_index("band")
    cos_table, sin_table = dft_tables(length)
    wide = wide_table(cos_table, sin_table)
    freq_x, freq_y, freq_z = (gvectors[0], gvectors[1], gvectors[2])
    norm_factor = float(length) ** (-1.5)
    pairs_all = ROUNDS * val_dev * cond_dev * lax.axis_size("band")
    cond_numbers = jnp.arange(cond_energy.shape[0], dtype=jnp.int32)
    cond_levels = jnp.sum(
        jnp.where(cond_band[:, None] == cond_numbers[None, :], cond_energy[None, :], 0.0), axis=1
    )
    cond_f = conduction.astype(jnp.float32)[None]
    local_y = freq_y - grid_pos * y_local
    inside = (local_y >= 0) & (local_y < y_local)
    local_y = jnp.clip(local_y, 0, y_local - 1)
    elem_rounds = []
    weight_rounds = []
    for round_no in range(ROUNDS):
        owner_pos = owners[round_no]
        val_bands = from_root(valence, "band", owner_pos)
        val_levels = lax.dynamic_slice_in_dim(val_energy, owner_pos * val_dev, val_dev, 0)
        val_f = val_bands.astype(jnp.float32)[:, None]
        dens_re = val_f[:, :, 0] * cond_f[:, :, 0] + val_f[:, :, 1] * cond_f[:, :, 1]
        dens_im = val_f[:, :, 0] * cond_f[:, :, 1] - val_f[:, :, 1] * cond_f[:, :, 0]
        density = jnp.concatenate([dens_re, dens_im], axis=-1).astype(jnp.bfloat16)
        density = density.reshape(val_dev * cond_dev, x_local, length, 2 * length)
        plane = plane_transform(density, wide, cos_table, sin_table)
        block = lax.all_to_all(plane, "grid", split_axis=2, concat_axis=1, tiled=True)
        cos_part = jnp.einsum("bxyk,xq->bqyk", block, cos_table, preferred_element_type=jnp.float32)
        sin_part = jnp.einsum("bxyk,xq->bqyk", block, sin_table, preferred_element_type=jnp.float32)
        full_re = cos_part[..., :length] + sin_part[..., length:]
        full_im = cos_part[..., length:] - sin_part[..., :length]
        elem_re = jnp.where(inside[None, :], full_re[:, freq_x, local_y, freq_z], 0.0) * norm_factor
        elem_im = jnp.where(inside[None, :], full_im[:, freq_x, local_y, freq_z], 0.0) * norm_factor
        elem_round = jnp.stack([elem_re, elem_im], axis=1)
        elem_rounds.append(elem_round)
        pair_weight = 2.0 / (pairs_all * (val_levels[:, None] - cond_levels[None, :]))
        weight_rounds.append(pair_weight.reshape(val_dev * cond_dev))
    local_elements = jnp.concatenate(elem_rounds, axis=0)
    local_weights = jnp.concatenate(weight_rounds, axis=0)
    summed = lax.psum(local_elements, "grid")
    row_count = summed.shape[2] // lax.axis_size("grid")
    col_count = summed.shape[2] // lax.axis_size("band")
    gathered, all_weights = (
        lax.all_gather(summed, "band", axis=0, tiled=True),
        lax.all_gather(local_weights, "band", axis=0, tiled=True),
    )
    row_block = lax.dynamic_slice_in_dim(gathered, grid_pos * row_count, row_count, 2)
    col_block = lax.dynamic_slice_in_dim(gathered, band_pos * col_count, col_count, 2)
    weighted = row_block * all_weights[:, None, None]
    right_side = jnp.concatenate([col_block[:, 0], col_block[:, 1]], axis=0)
    left_real = jnp.concatenate([weighted[:, 0], weighted[:, 1]], axis=0)
    left_imag = jnp.concatenate([weighted[:, 1], -weighted[:, 0]], axis=0)
    high = lax.Precision.HIGHEST
    chi_re = jnp.einsum("pr,pc->rc", left_real, right_side, precision=high)
    chi_im = jnp.einsum("pr,pc->rc", left_imag, right_side, precision=high)
    return jnp.stack([chi_re, chi_im])


def solution(mesh):
    return jax.shard_map(
        shards,
        mesh=mesh,
        in_specs=(
            P("band", None, "grid", None, None),
            P("band", None, "grid", None, None),
            P(),
            P(),
            P("band"),
            P(),
            P(),
        ),
        out_specs=P(None, "grid", "band"),
        check_vma=False,
    )
```

profile of v0, /device:TPU:1, one launch (start us, length us, event | category | flops | bytes accessed | tf_op | source)
XLA Modules:
  0.0 955.0 jit_solution(14158442999222053255)
XLA Ops:
  6.5 1.3 fusion.101
  9.2 8.4 select_bitcast_fusion.1
  17.7 0.7 fusion.57
  18.3 0.7 sine_convert_fusion
  19.0 0.6 copy-done.6
  19.6 0.8 bitcast_convert_fusion
  20.4 2.1 slice_bitcast_fusion.5
  22.5 287.6 %all-reduce.7.cloned.1.call-done = (bf16[2,1,2,20,160,160]{5,4,3,0,2,1:T(8,128)(2,1)}, bf16[2,1,2,20,160,160]{5,4,3,0,2,1:T(8,128)(2,1)}) async-done(((bf16[2,1,2,20,160,160]{5,4,3,0,2,1:T(8,128)(2,1)}, bf16[2,1,2,20,160,160]{5,4,3,0,2,1:T(8,128)(2,1)}), (bf16[2,1,2,20,160,160]{5,4,3,0,2,1:T(8,128)(2,1)}, bf16[2,1,2,20,160,160]{5,4,3,0,2,1:T(8,128)(2,1)})) %all-reduce.7.cloned.1.call-update) | async-done | bytes 8192016 | tf_op jit(solution)/shard_map/psum | solution.py:12
  310.1 9.6 %broadcast_in_dim.74 = f32[2,1,2,20,160,160]{5,4,3,0,2,1:T(8,128)} convert(bf16[2,1,2,20,160,160]{5,4,3,0,2,1:T(8,128)(2,1)} %get-tuple-element.6) | non-fusion elementwise | flops 2048000 | bytes 12288000 | tf_op jit(solution)/shard_map/broadcast_in_dim | solution.py:67
  319.7 6.6 broadcast_in_dim.79
  326.4 16.5 %add_convert_fusion.1 = (bf16[2,20,160,160]{3,2,1,0:T(8,128)(2,1)}, bf16[2,20,160,160]{3,2,1,0:T(8,128)(2,1)}, bf16[2,20,160,160]{3,2,1,0:T(8,128)(2,1)}, bf16[2,20,160,160]{3,2,1,0:T(8,128)(2,1)}) fusion(f32[2,1,2,20,160,160]{5,4,3,0,2,1:T(8,128)} %broadcast_in_dim.74, f32[20,160,160]{2,1,0:T(8,128)} %get-tuple-element.22, ...), kind=kLoop, calls=%fused_computation.24 | loop fusion | flops 16384000 | bytes 28672000 | tf_op jit(solution)/shard_map/convert.9
  342.8 6.2 fusion.32
  349.1 2.2 copy-done.3
  351.3 2.1 convolution_bitcast_fusion
  353.4 4.5 convolution_bitcast_fusion.1
  357.8 6.1 fusion.1
  363.9 6.9 pad_maximum_fusion.1
  370.8 9.7 %copy.88 = bf16[2,20,160,320]{3,0,1,2:T(2,128)(2,1)} copy(bf16[2,20,160,320]{3,2,1,0:T(8,128)(2,1)} %pad_maximum_fusion.1) | data formatting | bytes 8192000 | tf_op jit(solution)/shard_map/concatenate | solution.py:37
  380.5 7.1 all-to-all-start.1
  387.6 5.2 fusion.35
  392.9 2.3 copy-done.2
  395.1 2.1 convolution_bitcast_fusion.2
  397.2 4.5 convolution_bitcast_fusion.3
  401.7 6.0 fusion.3
  407.7 6.9 pad_maximum_fusion
  414.7 9.7 %copy.76 = bf16[2,20,160,320]{3,0,1,2:T(2,128)(2,1)} copy(bf16[2,20,160,320]{3,2,1,0:T(8,128)(2,1)} %pad_maximum_fusion) | data formatting | bytes 8192000 | tf_op jit(solution)/shard_map/concatenate | solution.py:37
  424.4 30.3 %all-to-all-done.1 = bf16[2,20,160,320]{3,0,1,2:T(2,128)(2,1)} async-done(((bf16[2,20,160,320]{3,0,1,2:T(2,128)(2,1)}), bf16[2,20,160,320]{3,0,1,2:T(2,128)(2,1)}, u32[]{:S(2)}, u32[]{:S(2)}) %all-to-all-start.1) | async-done | bytes 4096032 | tf_op jit(solution)/shard_map/all_to_all | solution.py:73
  454.7 4.6 all-to-all-start
  459.4 0.4 all-reduce.5.cloned.1.call-start
  459.8 0.1 and_reduce_fusion
  459.9 0.1 fusion.65
  460.1 7.9 copy.90
  468.0 8.3 fusion.26
  476.3 5.8 fusion.29
  482.1 46.0 %all-to-all-done = bf16[2,20,160,320]{3,0,1,2:T(2,128)(2,1)} async-done(((bf16[2,20,160,320]{3,0,1,2:T(2,128)(2,1)}), bf16[2,20,160,320]{3,0,1,2:T(2,128)(2,1)}, u32[]{:S(2)}, u32[]{:S(2)}) %all-to-all-start) | async-done | bytes 4096032 | tf_op jit(solution)/shard_map/all_to_all | solution.py:73
  528.1 8.0 copy.78
  536.2 8.7 fusion.20
  544.9 5.8 fusion.23
  550.7 9.4 slice_add_fusion
  560.1 10.7 %copy.96 = f32[2,160,20,160]{3,0,2,1:T(2,128)} copy(f32[2,160,20,160]{3,1,2,0:T(8,128)} %get-tuple-element.14) | data formatting | bytes 8192000 | tf_op jit(solution)/shard_map/sub | solution.py:77
  570.7 10.6 %copy.95 = f32[2,160,20,160]{3,0,2,1:T(2,128)} copy(f32[2,160,20,160]{3,1,2,0:T(8,128)} %get-tuple-element.13) | data formatting | bytes 8192000 | tf_op jit(solution)/shard_map/add | solution.py:76
  581.4 51.3 %gather_fusion.3 = f32[4096,2]{0,1:T(2,128)S(1)} fusion(f32[2,160,20,160]{3,0,2,1:T(2,128)} %copy.96, s32[4096]{0:T(1024)S(1)} %bitcast.147), kind=kCustom, calls=%fused_computation.3 | custom fusion | bytes 114688 | tf_op jit(solution)/shard_map/gather | solution.py:79
  632.7 51.4 %gather_fusion.2 = f32[4096,2]{0,1:T(2,128)S(1)} fusion(f32[2,160,20,160]{3,0,2,1:T(2,128)} %copy.95, s32[4096]{0:T(1024)S(1)} %bitcast.148), kind=kCustom, calls=%fused_computation.2 | custom fusion | bytes 114688 | tf_op jit(solution)/shard_map/gather | solution.py:78
  684.1 15.4 %slice_add_fusion.2 = (f32[2,160,20,160]{3,1,2,0:T(8,128)}, f32[2,160,20,160]{3,1,2,0:T(8,128)}) fusion(f32[2,160,20,320]{3,1,2,0:T(8,128)} %fusion.23, f32[2,160,20,320]{3,1,2,0:T(8,128)} %fusion.20), kind=kLoop, calls=%fused_computation.13 | loop fusion | flops 2048000 | bytes 24576000 | tf_op jit(solution)/shard_map/add | solution.py:76
  699.5 10.7 %copy.84 = f32[2,160,20,160]{3,0,2,1:T(2,128)} copy(f32[2,160,20,160]{3,1,2,0:T(8,128)} %get-tuple-element.8) | data formatting | bytes 8192000 | tf_op jit(solution)/shard_map/sub | solution.py:77
  710.2 51.6 %gather_fusion.1 = f32[4096,2]{0,1:T(2,128)S(1)} fusion(f32[2,160,20,160]{3,0,2,1:T(2,128)} %copy.84, s32[4096]{0:T(1024)S(1)} %bitcast.149), kind=kCustom, calls=%fused_computation.1 | custom fusion | bytes 114688 | tf_op jit(solution)/shard_map/gather | solution.py:79
  761.8 10.7 %copy.83 = f32[2,160,20,160]{3,0,2,1:T(2,128)} copy(f32[2,160,20,160]{3,1,2,0:T(8,128)} %get-tuple-element.7) | data formatting | bytes 8192000 | tf_op jit(solution)/shard_map/add | solution.py:76
  772.4 51.3 %gather_fusion = f32[4096,2]{0,1:T(2,128)S(1)} fusion(f32[2,160,20,160]{3,0,2,1:T(2,128)} %copy.83, s32[4096]{0:T(1024)S(1)} %bitcast.150), kind=kCustom, calls=%fused_computation | custom fusion | bytes 114688 | tf_op jit(solution)/shard_map/gather | solution.py:78
  823.8 0.1 fusion.61
  823.9 0.7 maximum_maximum_fusion
  824.6 0.0 all-gather.2.cloned.1.call-start
  824.6 79.3 %all-reduce.5.cloned.1.call-done = f32[4,2,4096]{2,0,1:T(4,128)} async-done(((f32[4,2,4096]{2,0,1:T(4,128)}), f32[4,2,4096]{2,0,1:T(4,128)}) %all-reduce.5.cloned.1.call-update) | async-done | bytes 131088 | tf_op jit(solution)/shard_map/psum | solution.py:86
  903.9 1.7 copy.97
  907.6 0.7 dynamic-slice
  908.9 0.6 fusion.78
  909.5 0.7 multiply_divide_fusion.1
  910.2 0.2 maximum_dynamic-update-slice_fusion
  910.4 32.7 %all-reduce = f32[64]{0:T(128)S(1)} all-reduce(f32[64]{0:T(128)S(1)} %maximum_dynamic-update-slice_fusion), channel_id=1, replica_groups=mesh['band'=16,'grid'=8] {'band'}, use_global_device_ids=true, to_apply=%add | all-reduce | flops 64 | bytes 512
  943.1 1.1 dynamic-slice_multiply_fusion
  944.2 0.2 fusion.100
  944.5 1.2 constant_dynamic-slice_fusion
  945.7 0.6 convolution_bitcast_fusion.5
  946.3 0.6 convolution_bitcast_fusion.4
  947.0 1.0 pad_maximum_fusion.2
  (37 shorter events, 0.2 us)
Async XLA Ops:
  6.5 303.6 %all-reduce.7.cloned.1.call-start = ((), (), s32[]{:S(2)}) async-start(), calls=%async_computation.4 | async-start | bytes 26214400 | tf_op jit(solution)/shard_map/psum | solution.py:12
  17.6 1.9 copy-start.6
  310.1 9.6 %copy-start.4 = (bf16[2,1,2,20,160,160]{5,4,3,0,2,1:T(8,128)(2,1)S(1)}, bf16[2,1,2,20,160,160]{5,4,3,0,2,1:T(8,128)(2,1)}, u32[]{:S(2)}) copy-start(bf16[2,1,2,20,160,160]{5,4,3,0,2,1:T(8,128)(2,1)} %get-tuple-element.5) | copy-start | bytes 12288004
  349.1 2.2 copy-start.3
  380.5 7.1 copy-start.5
  380.5 74.2 %all-to-all-start.1 = ((bf16[2,20,160,320]{3,0,1,2:T(2,128)(2,1)}), bf16[2,20,160,320]{3,0,1,2:T(2,128)(2,1)}, u32[]{:S(2)}, u32[]{:S(2)}) async-start(bf16[2,20,160,320]{3,0,1,2:T(2,128)(2,1)} %copy.88), calls=%async_computation.1 | async-start | bytes 9830400 | tf_op jit(solution)/shard_map/all_to_all | solution.py:73
  392.9 2.3 copy-start.2
  424.4 35.5 %copy-start.7 = (s32[3,4096]{1,0:T(4,128)S(1)}, s32[3,4096]{1,0:T(4,128)}, u32[]{:S(2)}) copy-start(s32[3,4096]{1,0:T(4,128)} %param.13) | copy-start | bytes 147460
  454.7 73.4 %all-to-all-start = ((bf16[2,20,160,320]{3,0,1,2:T(2,128)(2,1)}), bf16[2,20,160,320]{3,0,1,2:T(2,128)(2,1)}, u32[]{:S(2)}, u32[]{:S(2)}) async-start(bf16[2,20,160,320]{3,0,1,2:T(2,128)(2,1)} %copy.76), calls=%async_computation | async-start | bytes 9830400 | tf_op jit(solution)/shard_map/all_to_all | solution.py:73
  459.4 444.6 %all-reduce.5.cloned.1.call-start = ((), (), s32[]{:S(2)}) async-start(), calls=%async_computation.2 | async-start | bytes 262144 | tf_op jit(solution)/shard_map/psum | solution.py:86
  468.0 8.3 copy-start
  536.2 8.7 copy-start.1
  536.2 14.5 %slice-start = ((s8[9830400]{0:T(1024)(128)(4,1)}), s8[4194304]{0:T(1024)(128)(4,1)S(1)}, s32[]{:S(2)}) async-start(s8[9830400]{0:T(1024)(128)(4,1)} %bitcast.151), calls=%async_computation.5 | async-start | bytes 8388608
  536.2 14.5 %slice-start.1 = ((s8[9830400]{0:T(1024)(128)(4,1)}), s8[4194304]{0:T(1024)(128)(4,1)S(1)}, s32[]{:S(2)}) async-start(s8[9830400]{0:T(1024)(128)(4,1)} %bitcast.151), calls=%async_computation.6 | async-start | bytes 8388608
  544.9 5.8 slice-start.2
  772.4 135.2 %copy-start.10 = (u32[128]{0:T(128)S(1)}, u32[128]{0:T(128)}, u32[]{:S(2)}) copy-start(u32[128]{0:T(128)} %constant.132) | copy-start | bytes 1540
  772.4 136.5 %copy-start.9 = (f32[16]{0:T(128)S(1)}, f32[16]{0:T(128)}, u32[]{:S(2)}) copy-start(f32[16]{0:T(128)} %param.10) | copy-start | bytes 196
  772.4 137.1 %copy-start.8 = (f32[32]{0:T(128)S(1)}, f32[32]{0:T(128)}, u32[]{:S(2)}) copy-start(f32[32]{0:T(128)} %param.9) | copy-start | bytes 388
  824.6 118.5 %all-gather.2.cloned.1.call-start = ((), (), s32[]{:S(2)}) async-start(), calls=%async_computation.3 | async-start | bytes 2228224 | tf_op jit(solution)/shard_map/all_gather | solution.py:90
Sparse Core Ops, SparseCore 0:
  17.8 292.2 all-reduce.6
  824.7 79.1 all-reduce.4
  905.8 37.2 all-gather.1
where the time goes:
time: 963 us; the launch traced here: 955 us
  waiting for transfers between devices  443 us (46%)
  local copies, waits for them, and re-layouts  296 us (31%)
  other arithmetic  98.7 us (10%)
  matrix products  54.4 us (6%)
  blocking collectives  32.7 us (3%)
  between operations  17.7 us (2%)
  starting transfers between devices  12.2 us (1%)
    psum x1, waiting for transfers between devices, from_root(): return lax.psum(block, axis)  288 us
    gather x2, local copies, waits for them, and re-layouts, shards(): full_im[:, freq_x, local_y, freq_z]  103 us
    gather x2, local copies, waits for them, and re-layouts, shards(): full_re[:, freq_x, local_y, freq_z]  103 us
    psum x1, waiting for transfers between devices, shards(): summed = lax.psum(local_elements, 'grid')  79.3 us
    all_to_all x2, waiting for transfers between devices, shards(): lax.all_to_all(plane, 'grid', split_axis=2, concat_axis=1, tiled=True)  76.4 us
    unnamed x1, blocking collectives  32.7 us
    another operation x3, other arithmetic  28.6 us
    add x2, other arithmetic, shards(): full_re = cos_part[..., :length] + sin_part[..., length:]  24.8 us
  transfers between devices with their start and end apart: 5, of which 4 were waited for; matrix products, arithmetic and copies ran while one was open for 7% of the time, Pallas kernels for 0%

commit v1 on v0

--- a/solution.py
+++ b/solution.py
@@ -70,7 +70,10 @@
         density = jnp.concatenate([dens_re, dens_im], axis=-1).astype(jnp.bfloat16)
         density = density.reshape(val_dev * cond_dev, x_local, length, 2 * length)
         plane = plane_transform(density, wide, cos_table, sin_table)
-        block = lax.all_to_all(plane, "grid", split_axis=2, concat_axis=1, tiled=True)
+        n_dev = lax.axis_size("grid")
+        blocks = jnp.stack(jnp.split(plane, n_dev, axis=2), axis=0)
+        blocks = lax.all_to_all(blocks, "grid", split_axis=0, concat_axis=0)
+        block = jnp.concatenate(blocks, axis=1)
         cos_part = jnp.einsum("bxyk,xq->bqyk", block, cos_table, preferred_element_type=jnp.float32)
         sin_part = jnp.einsum("bxyk,xq->bqyk", block, sin_table, preferred_element_type=jnp.float32)
         full_re = cos_part[..., :length] + sin_part[..., length:]

time: 963 us -> 959 us (level)
  local copies, waits for them, and re-layouts: 296 us -> 275 us
    concatenate x2 -> x0, local copies, waits for them, and re-layouts: 19.4 us -> none  [plane_transform(): return jnp.concatenate([real_part, imag_part], axis=-1).astype(jnp.bfloat16)]
    another operation x0 -> x2, local copies, waits for them, and re-layouts: none -> 19.3 us  [shards(): blocks = jnp.stack(jnp.split(plane, n_dev, axis=2), axis=0)]
    unnamed x2 -> x16, other arithmetic: 0.16 us -> 18.4 us
    all_to_all x2 -> x0, local copies, waits for them, and re-layouts: 16 us -> none  [shards(): lax.all_to_all(plane, 'grid', split_axis=2, concat_axis=1, tiled=True)]
    concatenate x2 -> x0, other arithmetic: 13.9 us -> none  [plane_transform(): return jnp.concatenate([real_part, imag_part], axis=-1).astype(jnp.bfloat16)]
    another operation x3 -> x5, other arithmetic: 28.6 us -> 33.5 us
  transfers between devices with their start and end apart: 5 -> 5, of which waited for: 4 -> 5; matrix products, arithmetic and copies ran while one was open for 7% -> 7% of each run, Pallas kernels for 0% -> 0%
where the time goes in v1:
time: 959 us; the launch traced here: 952 us
  waiting for transfers between devices  445 us (46%)
  local copies, waits for them, and re-layouts  275 us (29%)
  other arithmetic  108 us (11%)
  matrix products  61.7 us (6%)
  blocking collectives  32.6 us (3%)
  between operations  17.4 us (2%)
  starting transfers between devices  11.7 us (1%)
    psum x1, waiting for transfers between devices, from_root(): return lax.psum(block, axis)  288 us
    gather x2, local copies, waits for them, and re-layouts, shards(): full_re[:, freq_x, local_y, freq_z]  103 us
    gather x2, local copies, waits for them, and re-layouts, shards(): full_im[:, freq_x, local_y, freq_z]  103 us
    psum x1, waiting for transfers between devices, shards(): summed = lax.psum(local_elements, 'grid')  79 us
    all_to_all x2, waiting for transfers between devices, shards(): blocks = lax.all_to_all(blocks, 'grid', split_axis=0, concat_axis=0)  78.4 us
    unnamed x1, blocking collectives  32.6 us
    another operation x3, other arithmetic  30.7 us
    broadcast_in_dim x3, other arithmetic, shards(): val_f = val_bands.astype(jnp.float32)[:, None]  24.7 us
  transfers between devices with their start and end apart: 5, of which 5 were waited for; matrix products, arithmetic and copies ran while one was open for 7% of the time, Pallas kernels for 0%

profile of v1, /device:TPU:1, one launch (start us, length us, event | category | flops | bytes accessed | tf_op | source)
XLA Modules:
  0.0 952.0 jit_solution(14372033686617017076)
XLA Ops:
  6.5 1.3 fusion.119
  9.1 8.4 select_bitcast_fusion.1
  17.6 0.7 fusion.75
  18.3 0.7 sine_convert_fusion
  19.5 0.8 bitcast_convert_fusion
  20.3 2.1 slice_bitcast_fusion.5
  22.4 287.6 %all-reduce.7.cloned.1.call-done = (bf16[2,1,2,20,160,160]{5,4,3,0,2,1:T(8,128)(2,1)}, bf16[2,1,2,20,160,160]{5,4,3,0,2,1:T(8,128)(2,1)}) async-done(((bf16[2,1,2,20,160,160]{5,4,3,0,2,1:T(8,128)(2,1)}, bf16[2,1,2,20,160,160]{5,4,3,0,2,1:T(8,128)(2,1)}), (bf16[2,1,2,20,160,160]{5,4,3,0,2,1:T(8,128)(2,1)}, bf16[2,1,2,20,160,160]{5,4,3,0,2,1:T(8,128)(2,1)})) %all-reduce.7.cloned.1.call-update) | async-done | bytes 8192016 | tf_op jit(solution)/shard_map/psum | solution.py:12
  310.1 9.6 %broadcast_in_dim.74 = f32[2,1,2,20,160,160]{5,4,3,0,2,1:T(8,128)} convert(bf16[2,1,2,20,160,160]{5,4,3,0,2,1:T(8,128)(2,1)} %get-tuple-element.6) | non-fusion elementwise | flops 2048000 | bytes 12288000 | tf_op jit(solution)/shard_map/broadcast_in_dim | solution.py:67
  319.7 6.7 broadcast_in_dim.79
  326.3 16.6 %add_convert_fusion.1 = (bf16[2,20,160,160]{3,2,1,0:T(8,128)(2,1)}, bf16[2,20,160,160]{3,2,1,0:T(8,128)(2,1)}, bf16[2,20,160,160]{3,2,1,0:T(8,128)(2,1)}, bf16[2,20,160,160]{3,2,1,0:T(8,128)(2,1)}) fusion(f32[2,1,2,20,160,160]{5,4,3,0,2,1:T(8,128)} %broadcast_in_dim.74, f32[20,160,160]{2,1,0:T(8,128)} %get-tuple-element.22, ...), kind=kLoop, calls=%fused_computation.24 | loop fusion | flops 16384000 | bytes 28672000 | tf_op jit(solution)/shard_map/convert.9
  342.9 6.2 fusion.32
  349.2 2.1 convolution_bitcast_fusion
  351.3 5.9 convolution_bitcast_fusion.1
  357.1 6.9 fusion.1
  364.1 1.2 bitcast_dynamic-update-slice_fusion.6
  365.3 1.5 bitcast_dynamic-update-slice_fusion.5
  366.7 1.2 bitcast_dynamic-update-slice_fusion.4
  367.9 1.5 bitcast_dynamic-update-slice_fusion.3
  369.4 1.2 bitcast_dynamic-update-slice_fusion.2
  370.5 1.5 bitcast_dynamic-update-slice_fusion.1
  372.0 1.2 bitcast_dynamic-update-slice_fusion
  373.2 1.4 fusion.53
  374.6 9.6 %copy.55 = bf16[8,2,20,20,320]{4,1,3,2,0:T(2,128)(2,1)} copy(bf16[8,2,20,20,320]{4,3,2,1,0:T(8,128)(2,1)} %fusion.53) | data formatting | bytes 8192000 | tf_op jit(solution)/shard_map/stack | solution.py:74
  384.2 6.8 all-to-all-start.1
  391.1 5.2 fusion.35
  396.3 2.1 convolution_bitcast_fusion.2
  398.4 5.9 convolution_bitcast_fusion.3
  404.3 7.2 fusion.3
  411.5 1.2 bitcast_dynamic-update-slice_fusion.13
  412.7 1.5 bitcast_dynamic-update-slice_fusion.12
  414.1 1.2 bitcast_dynamic-update-slice_fusion.11
  415.3 1.5 bitcast_dynamic-update-slice_fusion.10
  416.8 1.2 bitcast_dynamic-update-slice_fusion.9
  417.9 1.5 bitcast_dynamic-update-slice_fusion.8
  419.4 1.2 bitcast_dynamic-update-slice_fusion.7
  420.6 1.4 fusion.55
  422.0 9.7 %copy.45 = bf16[8,2,20,20,320]{4,1,3,2,0:T(2,128)(2,1)} copy(bf16[8,2,20,20,320]{4,3,2,1,0:T(8,128)(2,1)} %fusion.55) | data formatting | bytes 8192000 | tf_op jit(solution)/shard_map/stack | solution.py:74
  431.7 26.5 %all-to-all-done.1 = bf16[8,2,20,20,320]{4,1,3,2,0:T(2,128)(2,1)} async-done(((bf16[8,2,20,20,320]{4,1,3,2,0:T(2,128)(2,1)}), bf16[8,2,20,20,320]{4,1,3,2,0:T(2,128)(2,1)}, u32[]{:S(2)}, u32[]{:S(2)}) %all-to-all-start.1) | async-done | bytes 4096032 | tf_op jit(solution)/shard_map/all_to_all | solution.py:75
  458.2 4.6 all-to-all-start
  463.3 8.2 fusion.26
  471.5 8.2 fusion.29
  479.7 51.9 %all-to-all-done = bf16[8,2,20,20,320]{4,1,3,2,0:T(2,128)(2,1)} async-done(((bf16[8,2,20,20,320]{4,1,3,2,0:T(2,128)(2,1)}), bf16[8,2,20,20,320]{4,1,3,2,0:T(2,128)(2,1)}, u32[]{:S(2)}, u32[]{:S(2)}) %all-to-all-start) | async-done | bytes 4096032 | tf_op jit(solution)/shard_map/all_to_all | solution.py:75
  531.6 8.3 fusion.20
  539.9 8.4 fusion.23
  548.3 9.5 %slice_add_fusion = (f32[2,160,20,160]{3,1,2,0:T(8,128)}, f32[2,160,20,160]{3,1,2,0:T(8,128)}) fusion(f32[2,160,20,320]{3,1,2,0:T(8,128)} %fusion.29, f32[2,160,20,320]{3,1,2,0:T(8,128)S(1)} %bitcast.186), kind=kLoop, calls=%fused_computation.5 | loop fusion | flops 2048000 | bytes 24576000 | tf_op jit(solution)/shard_map/add | solution.py:79
  557.9 10.7 %copy.61 = f32[2,160,20,160]{3,0,2,1:T(2,128)} copy(f32[2,160,20,160]{3,1,2,0:T(8,128)} %get-tuple-element.14) | data formatting | bytes 8192000 | tf_op jit(solution)/shard_map/sub | solution.py:80
  568.6 10.6 %copy.60 = f32[2,160,20,160]{3,0,2,1:T(2,128)} copy(f32[2,160,20,160]{3,1,2,0:T(8,128)} %get-tuple-element.13) | data formatting | bytes 8192000 | tf_op jit(solution)/shard_map/add | solution.py:79
  579.2 51.3 %gather_fusion.3 = f32[4096,2]{0,1:T(2,128)S(1)} fusion(f32[2,160,20,160]{3,0,2,1:T(2,128)} %copy.61, s32[4096]{0:T(1024)S(1)} %bitcast.181), kind=kCustom, calls=%fused_computation.3 | custom fusion | bytes 114688 | tf_op jit(solution)/shard_map/gather | solution.py:82
  630.6 51.6 %gather_fusion.2 = f32[4096,2]{0,1:T(2,128)S(1)} fusion(f32[2,160,20,160]{3,0,2,1:T(2,128)} %copy.60, s32[4096]{0:T(1024)S(1)} %bitcast.182), kind=kCustom, calls=%fused_computation.2 | custom fusion | bytes 114688 | tf_op jit(solution)/shard_map/gather | solution.py:81
  682.1 15.0 %slice_add_fusion.2 = (f32[2,160,20,160]{3,1,2,0:T(8,128)}, f32[2,160,20,160]{3,1,2,0:T(8,128)}) fusion(f32[2,160,20,320]{3,1,2,0:T(8,128)} %fusion.23, f32[2,160,20,320]{3,1,2,0:T(8,128)} %fusion.20), kind=kLoop, calls=%fused_computation.13 | loop fusion | flops 2048000 | bytes 24576000 | tf_op jit(solution)/shard_map/add | solution.py:79
  697.1 10.6 %copy.51 = f32[2,160,20,160]{3,0,2,1:T(2,128)} copy(f32[2,160,20,160]{3,1,2,0:T(8,128)} %get-tuple-element.8) | data formatting | bytes 8192000 | tf_op jit(solution)/shard_map/sub | solution.py:80
  707.7 51.5 %gather_fusion.1 = f32[4096,2]{0,1:T(2,128)S(1)} fusion(f32[2,160,20,160]{3,0,2,1:T(2,128)} %copy.51, s32[4096]{0:T(1024)S(1)} %bitcast.183), kind=kCustom, calls=%fused_computation.1 | custom fusion | bytes 114688 | tf_op jit(solution)/shard_map/gather | solution.py:82
  759.3 10.6 %copy.50 = f32[2,160,20,160]{3,0,2,1:T(2,128)} copy(f32[2,160,20,160]{3,1,2,0:T(8,128)} %get-tuple-element.7) | data formatting | bytes 8192000 | tf_op jit(solution)/shard_map/add | solution.py:79
  769.9 51.4 %gather_fusion = f32[4096,2]{0,1:T(2,128)S(1)} fusion(f32[2,160,20,160]{3,0,2,1:T(2,128)} %copy.50, s32[4096]{0:T(1024)S(1)} %bitcast.184), kind=kCustom, calls=%fused_computation | custom fusion | bytes 114688 | tf_op jit(solution)/shard_map/gather | solution.py:81
  821.4 0.7 maximum_maximum_fusion
  822.2 79.0 %all-reduce.5.cloned.1.call-done = f32[4,2,4096]{2,0,1:T(4,128)} async-done(((f32[4,2,4096]{2,0,1:T(4,128)}), f32[4,2,4096]{2,0,1:T(4,128)}) %all-reduce.5.cloned.1.call-update) | async-done | bytes 131088 | tf_op jit(solution)/shard_map/psum | solution.py:89
  901.2 1.7 copy.62
  906.1 0.6 fusion.96
  906.7 0.7 multiply_divide_fusion.1
  907.6 32.6 %all-reduce = f32[64]{0:T(128)S(1)} all-reduce(f32[64]{0:T(128)S(1)} %maximum_dynamic-update-slice_fusion), channel_id=1, replica_groups=mesh['band'=16,'grid'=8] {'band'}, use_global_device_ids=true, to_apply=%add | all-reduce | flops 64 | bytes 512
  940.4 1.1 dynamic-slice_multiply_fusion
  941.7 1.2 constant_dynamic-slice_fusion
  943.0 0.6 convolution_bitcast_fusion.5
  944.2 1.0 pad_maximum_fusion
  (41 shorter events, 3.0 us)
Async XLA Ops:
  6.5 303.5 %all-reduce.7.cloned.1.call-start = ((), (), s32[]{:S(2)}) async-start(), calls=%async_computation.4 | async-start | bytes 26214400 | tf_op jit(solution)/shard_map/psum | solution.py:12
  17.6 1.9 copy-start.2
  310.1 9.6 %copy-start = (bf16[2,1,2,20,160,160]{5,4,3,0,2,1:T(8,128)(2,1)S(1)}, bf16[2,1,2,20,160,160]{5,4,3,0,2,1:T(8,128)(2,1)}, u32[]{:S(2)}) copy-start(bf16[2,1,2,20,160,160]{5,4,3,0,2,1:T(8,128)(2,1)} %get-tuple-element.5) | copy-start | bytes 12288004
  384.2 6.8 copy-start.1
  384.2 73.9 %all-to-all-start.1 = ((bf16[8,2,20,20,320]{4,1,3,2,0:T(2,128)(2,1)}), bf16[8,2,20,20,320]{4,1,3,2,0:T(2,128)(2,1)}, u32[]{:S(2)}, u32[]{:S(2)}) async-start(bf16[8,2,20,20,320]{4,1,3,2,0:T(2,128)(2,1)} %copy.55), calls=%async_computation.1 | async-start | bytes 9830400 | tf_op jit(solution)/shard_map/all_to_all | solution.py:75
  431.7 31.3 %copy-start.3 = (s32[3,4096]{1,0:T(4,128)S(1)}, s32[3,4096]{1,0:T(4,128)}, u32[]{:S(2)}) copy-start(s32[3,4096]{1,0:T(4,128)} %param.13) | copy-start | bytes 147460
  458.2 73.4 %all-to-all-start = ((bf16[8,2,20,20,320]{4,1,3,2,0:T(2,128)(2,1)}), bf16[8,2,20,20,320]{4,1,3,2,0:T(2,128)(2,1)}, u32[]{:S(2)}, u32[]{:S(2)}) async-start(bf16[8,2,20,20,320]{4,1,3,2,0:T(2,128)(2,1)} %copy.45), calls=%async_computation | async-start | bytes 9830400 | tf_op jit(solution)/shard_map/all_to_all | solution.py:75
  462.8 438.4 %all-reduce.5.cloned.1.call-start = ((), (), s32[]{:S(2)}) async-start(), calls=%async_computation.2 | async-start | bytes 262144 | tf_op jit(solution)/shard_map/psum | solution.py:89
  531.6 16.7 %slice-start = ((s8[9830400]{0:T(1024)(128)(4,1)}), s8[4194304]{0:T(1024)(128)(4,1)S(1)}, s32[]{:S(2)}) async-start(s8[9830400]{0:T(1024)(128)(4,1)} %bitcast.185), calls=%async_computation.5 | async-start | bytes 8388608
  531.6 16.7 %slice-start.1 = ((s8[9830400]{0:T(1024)(128)(4,1)}), s8[4194304]{0:T(1024)(128)(4,1)S(1)}, s32[]{:S(2)}) async-start(s8[9830400]{0:T(1024)(128)(4,1)} %bitcast.185), calls=%async_computation.6 | async-start | bytes 8388608
  539.9 8.4 slice-start.2
  769.9 134.9 %copy-start.6 = (u32[128]{0:T(128)S(1)}, u32[128]{0:T(128)}, u32[]{:S(2)}) copy-start(u32[128]{0:T(128)} %constant.132) | copy-start | bytes 1540
  769.9 136.2 %copy-start.5 = (f32[16]{0:T(128)S(1)}, f32[16]{0:T(128)}, u32[]{:S(2)}) copy-start(f32[16]{0:T(128)} %param.10) | copy-start | bytes 196
  769.9 136.8 %copy-start.4 = (f32[32]{0:T(128)S(1)}, f32[32]{0:T(128)}, u32[]{:S(2)}) copy-start(f32[32]{0:T(128)} %param.9) | copy-start | bytes 388
  822.1 118.2 %all-gather.2.cloned.1.call-start = ((), (), s32[]{:S(2)}) async-start(), calls=%async_computation.3 | async-start | bytes 2228224 | tf_op jit(solution)/shard_map/all_gather | solution.py:93
Sparse Core Ops, SparseCore 0:
  17.7 292.2 all-reduce.6
  822.2 78.9 all-reduce.4
  903.0 37.2 all-gather.1
